TPU v7x, 128 devices: a whole 4x4x4 slice. The times are simulated.
128 devices in a mesh: board: 32 (over x, y, core), hand: 4 (over z).
Axes of the slice: x: 4, y: 4, z: 4, core: 2. Of those that a mesh axis runs over, the one named last changes fastest.
Arguments:
- reach_pre: float32 [1408], P(('board', 'hand')), may hold values from 0.05 to 1
- strategy: bfloat16 [256, 128, 1408], P('board', None, 'hand'), may hold values from 0 to 1
- ranks: int32 [256, 8, 1408], P('board'), may hold values from 0 to 94
- boards: int32 [256, 8, 5], P('board'), may hold values from 0 to 51, as said below
- river_live: int32 [256], P('board'), may hold values from 1 to 8, as said below
- iso_weight: int32 [256], P('board'), may hold values from 1 to 24
- pot: float32 [128], replicated, may hold values from 2 to 24
- line_act: int32 [128], replicated, may hold values from 0 to 2
Outputs:
- preflop_value: float32 [1408], P('hand')
Inputs may be any that keep to these rules, and one draw needn't show every extreme that they name: `boards`: the five cards of a runout are distinct; all runouts of a flop share their first three cards. `river_live`: in every draw some flop has all 8 runouts live.
All inputs are finite; a program needn't handle non-finite values.
Results may differ from a plain program's by a relative error of at most 0.0003.
Values may be sent and summed in bfloat16 or wider, within the bound.
A program may use at most 64 MiB of HBM per device.

v0:
```python
import jax
import jax.numpy as jnp
import numpy as np
from jax import lax
from jax.sharding import PartitionSpec as P

HANDS = 1326
HPAD = 1408
ACTS = 3


def card_tables():
    first_card, second_card = np.triu_indices(52, 1)
    padding = HPAD - HANDS
    first_card = np.concatenate([first_card, np.full(padding, 52)]).astype(np.int32)
    second_card = np.concatenate([second_card, np.full(padding, 53)]).astype(np.int32)
    alive_mask = np.concatenate([np.ones(HANDS), np.zeros(padding)]).astype(np.float32)
    return (jnp.asarray(first_card), jnp.asarray(second_card), jnp.asarray(alive_mask))


def unblocked(first_rows, second_rows, first_cols, second_cols):
    clear = (first_rows[:, None] != first_cols[None, :]) & (
        first_rows[:, None] != second_cols[None, :]
    )
    clear = (
        clear
        & (second_rows[:, None] != first_cols[None, :])
        & (second_rows[:, None] != second_cols[None, :])
    )
    return clear.astype(jnp.float32)


def live_hands(first_card, second_card, alive_mask, board_cards):
    clear = jnp.all(
        (first_card[:, None] != board_cards[None, :])
        & (second_card[:, None] != board_cards[None, :]),
        axis=1,
    )
    return alive_mask * clear.astype(jnp.float32)


def showdown(rank_rows, rank_cols, live_rows, live_cols, blocking):
    signed = jnp.sign(rank_rows[:, None] - rank_cols[None, :]).astype(jnp.float32)
    return (signed * blocking.astype(jnp.float32) * live_rows[:, None] * live_cols[None, :]).astype(
        jnp.bfloat16
    )


def runout_sum(
    ranks_flop, boards_flop, count_flop, tables, row_span, col_span, blocking, reach_flop
):
    first_card, second_card, alive_mask = tables
    row_start, row_len = row_span
    col_start, col_len = col_span

    def add_runout(runout, acc, factor):
        rank_now = ranks_flop[runout]
        live_now = live_hands(first_card, second_card, alive_mask, boards_flop[runout])
        matrix = showdown(
            lax.dynamic_slice_in_dim(rank_now, row_start, row_len),
            rank_now,
            lax.dynamic_slice_in_dim(live_now, row_start, row_len),
            lax.dynamic_slice_in_dim(live_now, col_start, col_len),
            blocking,
        )
        values = lax.dot_general(
            matrix, reach_flop, (((1,), (1,)), ((), ())), preferred_element_type=jnp.float32
        )
        return acc + values * factor

    empty = jnp.zeros((row_len, reach_flop.shape[0]), jnp.float32)

    def every_step(runout, acc):
        return add_runout(runout, acc, (runout < count_flop).astype(jnp.float32))

    return lax.fori_loop(0, ranks_flop.shape[0], every_step, empty)


def body(reach_pre, strategy, ranks, boards, river_live, iso_weight, pot, line_act):
    tables = card_tables()
    first_card, second_card, alive_mask = tables
    full_reach = lax.all_gather(reach_pre, ("board", "hand"), axis=0, tiled=True)
    local_weight = jnp.sum(iso_weight.astype(jnp.float32))
    weight_total = lax.psum(local_weight, "board")
    total_reach = jnp.sum(full_reach * alive_mask)
    hand_rows = strategy.shape[2]
    slots = full_reach.shape[0]
    row_start = lax.axis_index("hand") * hand_rows
    own_first = lax.dynamic_slice_in_dim(first_card, row_start, hand_rows)
    own_second = lax.dynamic_slice_in_dim(second_card, row_start, hand_rows)
    own_reach = lax.dynamic_slice_in_dim(full_reach, row_start, hand_rows)
    line_reach = (own_reach[None, None, :] * strategy.astype(jnp.float32) / total_reach).astype(
        jnp.bfloat16
    )
    onehot = (line_act[:, None] == jnp.arange(ACTS, dtype=jnp.int32)[None, :]).astype(jnp.float32)
    flop_ids = jnp.arange(strategy.shape[0], dtype=jnp.int32)
    every_reach = lax.all_gather(line_reach, "hand", axis=2, tiled=True)
    blocking = unblocked(own_first, own_second, first_card, second_card).astype(jnp.bfloat16)

    def own_rows(flop_index):
        return runout_sum(
            ranks[flop_index],
            boards[flop_index],
            river_live[flop_index],
            tables,
            (row_start, hand_rows),
            (0, slots),
            blocking,
            every_reach[flop_index],
        )

    acc = lax.map(own_rows, flop_ids)
    line_values = acc * pot[None, None, :] / river_live.astype(jnp.float32)[:, None, None]
    group_values = jnp.dot(
        line_values, onehot, precision=lax.Precision.HIGHEST, preferred_element_type=jnp.float32
    )
    best = jnp.max(group_values, axis=2)
    partial_values = jnp.sum(iso_weight.astype(jnp.float32)[:, None] * best, axis=0)
    summed = lax.psum(partial_values, "board")
    return summed / weight_total


def solution(mesh):
    in_specs = (
        P(("board", "hand")),
        P("board", None, "hand"),
        P("board", None, None),
        P("board", None, None),
        P("board"),
        P("board"),
        P(),
        P(),
    )
    out_specs = P("hand")
    return jax.shard_map(body, mesh=mesh, in_specs=in_specs, out_specs=out_specs, check_vma=False)
```

profile of v0, /device:TPU:0, one launch (start us, length us, event | category | flops | bytes accessed | tf_op | source)
XLA Modules:
  0.0 370.8 jit_solution(5847999569311250122)
XLA Ops:
  7.5 68.2 %all-reduce = f32[1408]{0:T(1024)S(1)} all-reduce(f32[1408]{0:T(1024)S(1)} %dynamic-update-slice), channel_id=1, replica_groups=mesh['board'=32,'hand'=4] {'board','hand'}, use_global_device_ids=true, to_apply=%add | all-reduce | flops 1408 | bytes 11264
  75.8 1.3 multiply_reduce_fusion.1
  77.1 3.0 divide_convert_fusion
  80.9 33.0 %all-gather.2.cloned.1.call-done = bf16[8,128,1408]{1,0,2:T(8,128)(2,1)} async-done(((bf16[8,128,352]{1,0,2:T(8,128)(2,1)}), bf16[8,128,1408]{1,0,2:T(8,128)(2,1)}) %all-gather.2.cloned.1.call-update) | async-done | bytes 2883600 | tf_op jit(solution)/shard_map/all_gather | solution.py:97
  114.0 4.8 %copy.19 = bf16[8,128,1408]{2,1,0:T(8,128)(2,1)} copy(bf16[8,128,1408]{1,0,2:T(8,128)(2,1)} %all-gather.2.cloned.1.call-done) | data formatting | bytes 5767168
  118.8 175.5 %while.50 = (s32[]{:T(128)}, f32[8,352,128]{2,1,0:T(8,128)S(1)}, s32[8]{0:T(128)S(1)}, s32[8]{0:T(128)S(1)}, s32[8,8,1408]{2,1,0:T(8,128)}, /*index=5*/s32[8,8,5...) while((s32[]{:T(128)}, f32[8,352,128]{2,1,0:T(8,128)S(1)}, ...), condition=%wide.region_5.6_spmd.clone.clone, body=%wide.region_1.5_spmd.sunk.clone.clone.sunk | while | flops 135466512 | bytes 3946544 | solution.py:112
  121.5 1.0 dynamic-slice_bitcast_fusion.7
  125.5 15.2 %while.51 = (s32[]{:T(128)}, f32[352,128]{1,0:T(8,128)S(1)}, s32[8,1408]{1,0:T(8,128)S(1)}, s32[]{:T(128)}, bf16[352,1408]{1,0:T(8,128)(2,1)S(1)}, /*index=5*/s3...) while((s32[]{:T(128)}, f32[352,128]{1,0:T(8,128)S(1)}, ...), condition=%wide.region_4.4_spmd.clone.clone, body=%wide.region_2.0_spmd.sunk.clone.clone.sunk | while | flops 131005960 | bytes 1768713 | solution.py:76
  143.4 1.0 dynamic-slice_bitcast_fusion.7
  147.4 15.2 %while.51 = (s32[]{:T(128)}, f32[352,128]{1,0:T(8,128)S(1)}, s32[8,1408]{1,0:T(8,128)S(1)}, s32[]{:T(128)}, bf16[352,1408]{1,0:T(8,128)(2,1)S(1)}, /*index=5*/s3...) while((s32[]{:T(128)}, f32[352,128]{1,0:T(8,128)S(1)}, ...), condition=%wide.region_4.4_spmd.clone.clone, body=%wide.region_2.0_spmd.sunk.clone.clone.sunk | while | flops 131005960 | bytes 1768713 | solution.py:76
  165.4 1.0 dynamic-slice_bitcast_fusion.7
  169.4 15.2 %while.51 = (s32[]{:T(128)}, f32[352,128]{1,0:T(8,128)S(1)}, s32[8,1408]{1,0:T(8,128)S(1)}, s32[]{:T(128)}, bf16[352,1408]{1,0:T(8,128)(2,1)S(1)}, /*index=5*/s3...) while((s32[]{:T(128)}, f32[352,128]{1,0:T(8,128)S(1)}, ...), condition=%wide.region_4.4_spmd.clone.clone, body=%wide.region_2.0_spmd.sunk.clone.clone.sunk | while | flops 131005960 | bytes 1768713 | solution.py:76
  187.3 1.0 dynamic-slice_bitcast_fusion.7
  191.3 15.2 %while.51 = (s32[]{:T(128)}, f32[352,128]{1,0:T(8,128)S(1)}, s32[8,1408]{1,0:T(8,128)S(1)}, s32[]{:T(128)}, bf16[352,1408]{1,0:T(8,128)(2,1)S(1)}, /*index=5*/s3...) while((s32[]{:T(128)}, f32[352,128]{1,0:T(8,128)S(1)}, ...), condition=%wide.region_4.4_spmd.clone.clone, body=%wide.region_2.0_spmd.sunk.clone.clone.sunk | while | flops 131005960 | bytes 1768713 | solution.py:76
  209.3 1.0 dynamic-slice_bitcast_fusion.7
  213.2 15.2 %while.51 = (s32[]{:T(128)}, f32[352,128]{1,0:T(8,128)S(1)}, s32[8,1408]{1,0:T(8,128)S(1)}, s32[]{:T(128)}, bf16[352,1408]{1,0:T(8,128)(2,1)S(1)}, /*index=5*/s3...) while((s32[]{:T(128)}, f32[352,128]{1,0:T(8,128)S(1)}, ...), condition=%wide.region_4.4_spmd.clone.clone, body=%wide.region_2.0_spmd.sunk.clone.clone.sunk | while | flops 131005960 | bytes 1768713 | solution.py:76
  231.2 1.0 dynamic-slice_bitcast_fusion.7
  235.2 15.2 %while.51 = (s32[]{:T(128)}, f32[352,128]{1,0:T(8,128)S(1)}, s32[8,1408]{1,0:T(8,128)S(1)}, s32[]{:T(128)}, bf16[352,1408]{1,0:T(8,128)(2,1)S(1)}, /*index=5*/s3...) while((s32[]{:T(128)}, f32[352,128]{1,0:T(8,128)S(1)}, ...), condition=%wide.region_4.4_spmd.clone.clone, body=%wide.region_2.0_spmd.sunk.clone.clone.sunk | while | flops 131005960 | bytes 1768713 | solution.py:76
  253.1 1.0 dynamic-slice_bitcast_fusion.7
  257.1 15.2 %while.51 = (s32[]{:T(128)}, f32[352,128]{1,0:T(8,128)S(1)}, s32[8,1408]{1,0:T(8,128)S(1)}, s32[]{:T(128)}, bf16[352,1408]{1,0:T(8,128)(2,1)S(1)}, /*index=5*/s3...) while((s32[]{:T(128)}, f32[352,128]{1,0:T(8,128)S(1)}, ...), condition=%wide.region_4.4_spmd.clone.clone, body=%wide.region_2.0_spmd.sunk.clone.clone.sunk | while | flops 131005960 | bytes 1768713 | solution.py:76
  279.0 15.2 %while.51 = (s32[]{:T(128)}, f32[352,128]{1,0:T(8,128)S(1)}, s32[8,1408]{1,0:T(8,128)S(1)}, s32[]{:T(128)}, bf16[352,1408]{1,0:T(8,128)(2,1)S(1)}, /*index=5*/s3...) while((s32[]{:T(128)}, f32[352,128]{1,0:T(8,128)S(1)}, ...), condition=%wide.region_4.4_spmd.clone.clone, body=%wide.region_2.0_spmd.sunk.clone.clone.sunk | while | flops 131005960 | bytes 1768713 | solution.py:76
  294.3 1.1 fusion.7
  295.5 67.3 %all-reduce.1 = (f32[352]{0:T(512)S(1)}, f32[]{:T(128)}) all-reduce(f32[352]{0:T(512)S(1)} %multiply_reduce_fusion, f32[]{:T(128)} %convert_reduce_fusion), channel_id=1, replica_groups=mesh['board'=32,'hand'=4] {'board'}, use_global_device_ids=true, to_apply=%region_8.9 | all-reduce | flops 353 | bytes 2824 | tf_op jit(solution)/shard_map/psum | solution.py:119
  362.8 1.1 broadcast_divide_fusion
  (540 shorter events, 108.0 us)
Async XLA Ops:
  6.5 73.6 %copy-start = (s32[1408]{0:T(1024)S(1)}, s32[1408]{0:T(1024)}, u32[]{:S(2)}) copy-start(s32[1408]{0:T(1024)} %constant.188.clone) | copy-start | bytes 16900
  6.5 73.7 %copy-start.1 = (s32[1408]{0:T(1024)S(1)}, s32[1408]{0:T(1024)}, u32[]{:S(2)}) copy-start(s32[1408]{0:T(1024)} %constant.189.clone) | copy-start | bytes 16900
  6.5 73.8 %copy-start.4 = (s32[8]{0:T(128)S(1)}, s32[8]{0:T(128)}, u32[]{:S(2)}) copy-start(s32[8]{0:T(128)} %param.19) | copy-start | bytes 100
  6.5 73.8 %copy-start.3 = (s32[8]{0:T(128)S(1)}, s32[8]{0:T(128)}, u32[]{:S(2)}) copy-start(s32[8]{0:T(128)} %param.20) | copy-start | bytes 100
  6.5 107.4 %all-gather.2.cloned.1.call-start = ((), (), s32[]{:S(2)}) async-start(), calls=%async_computation | async-start | bytes 3604480 | tf_op jit(solution)/shard_map/all_gather | solution.py:97
  80.9 37.9 %copy-start.2 = (f32[1408]{0:T(1024)S(1)}, f32[1408]{0:T(1024)}, u32[]{:S(2)}) copy-start(f32[1408]{0:T(1024)} %constant.190.clone) | copy-start | bytes 16900
  118.8 175.5 %copy-start.5 = (f32[128]{0:T(128)S(1)}, f32[128]{0:T(128)}, u32[]{:S(2)}) copy-start(f32[128]{0:T(128)} %param.21) | copy-start | bytes 1540
  118.8 175.5 %copy-start.6 = (s32[128]{0:T(128)S(1)}, s32[128]{0:T(128)}, u32[]{:S(2)}) copy-start(s32[128]{0:T(128)} %param.22) | copy-start | bytes 1540
Sparse Core Ops, SparseCore 0:
  80.3 33.6 all-gather.1
where the time goes:
time: 373 us; the launch traced here: 371 us
  blocking collectives  136 us (36%)
  loops' own time  62.2 us (17%)
  matrix products  57.1 us (15%)
  local copies, waits for them, and re-layouts  50.9 us (14%)
  waiting for transfers between devices  33 us (9%)
  other arithmetic  18.5 us (5%)
  between operations  13.5 us (4%)
    unnamed x1, blocking collectives  68.2 us
    psum x1, blocking collectives, body(): summed = lax.psum(partial_values, 'board')  67.3 us
    dot_general x64, matrix products, add_runout(): lax.dot_general(matrix, reach_flop, (((1,), (1,)), ((), ())), preferred_e...  56 us
    another operation x8, loops' own time, runout_sum(): return lax.fori_loop(0, ranks_flop.shape[0], every_step, empty)  45.6 us
    all_gather x1, waiting for transfers between devices, body(): every_reach = lax.all_gather(line_reach, 'hand', axis=2, tiled=True)  33 us
    another operation x1, loops' own time, body(): acc = lax.map(own_rows, flop_ids)  16.6 us
    squeeze x8, local copies, waits for them, and re-layouts, own_rows(): every_reach[flop_index]  8.15 us
  transfers between devices with their start and end apart: 1, of which 1 were waited for; matrix products, arithmetic and copies ran while one was open for 0% of the time, Pallas kernels for 0%

commit v1 on v0

--- a/solution.py
+++ b/solution.py
@@ -116,7 +116,9 @@
     )
     best = jnp.max(group_values, axis=2)
     partial_values = jnp.sum(iso_weight.astype(jnp.float32)[:, None] * best, axis=0)
-    summed = lax.psum(partial_values, "board")
+    summed = partial_values
+    for hop in (1, 2, 4, 8, 16):
+        summed = summed + lax.ppermute(summed, "board", [(dev, dev ^ hop) for dev in range(32)])
     return summed / weight_total
 
 

time: 373 us -> 387 us (1.038)
  starting transfers between devices: 0.03 us -> 9.08 us
  waiting for transfers between devices: 33 us -> 41.1 us
  blocking collectives: 136 us -> 132 us
    ppermute x0 -> x5, starting transfers between devices: none -> 9.05 us  [body(): lax.ppermute(summed, 'board', [(dev, dev ^ hop) for dev in range(32)])]
    ppermute x0 -> x5, waiting for transfers between devices: none -> 7.43 us  [body(): lax.ppermute(summed, 'board', [(dev, dev ^ hop) for dev in range(32)])]
    psum x1, blocking collectives: 67.3 us -> 63.4 us  [body(): weight_total = lax.psum(local_weight, 'board')]
  transfers between devices with their start and end apart: 1 -> 6, of which waited for: 1 -> 5; matrix products, arithmetic and copies ran while one was open for 0% -> 0% of each run, Pallas kernels for 0% -> 0%
where the time goes in v1:
time: 387 us; the launch traced here: 384 us
  blocking collectives  132 us (34%)
  loops' own time  62.2 us (16%)
  matrix products  57.1 us (15%)
  local copies, waits for them, and re-layouts  50.9 us (13%)
  waiting for transfers between devices  41.1 us (11%)
  other arithmetic  18.7 us (5%)
  between operations  13.5 us (3%)
  starting transfers between devices  9.08 us (2%)
    unnamed x1, blocking collectives  68.2 us
    psum x1, blocking collectives, body(): weight_total = lax.psum(local_weight, 'board')  63.4 us
    dot_general x64, matrix products, add_runout(): lax.dot_general(matrix, reach_flop, (((1,), (1,)), ((), ())), preferred_e...  56 us
    another operation x8, loops' own time, runout_sum(): return lax.fori_loop(0, ranks_flop.shape[0], every_step, empty)  45.6 us
    all_gather x1, waiting for transfers between devices, body(): every_reach = lax.all_gather(line_reach, 'hand', axis=2, tiled=True)  33.6 us
    another operation x1, loops' own time, body(): acc = lax.map(own_rows, flop_ids)  16.6 us
    ppermute x5, starting transfers between devices, body(): lax.ppermute(summed, 'board', [(dev, dev ^ hop) for dev in range(32)])  9.05 us
    squeeze x8, local copies, waits for them, and re-layouts, own_rows(): every_reach[flop_index]  8.15 us
  transfers between devices with their start and end apart: 6, of which 5 were waited for; matrix products, arithmetic and copies ran while one was open for 0% of the time, Pallas kernels for 0%

profile of v1, /device:TPU:0, one launch (start us, length us, event | category | flops | bytes accessed | tf_op | source)
XLA Modules:
  0.0 384.1 jit_solution(13361338037906738749)
XLA Ops:
  7.5 68.2 %all-reduce = f32[1408]{0:T(1024)S(1)} all-reduce(f32[1408]{0:T(1024)S(1)} %dynamic-update-slice), channel_id=1, replica_groups=mesh['board'=32,'hand'=4] {'board','hand'}, use_global_device_ids=true, to_apply=%add | all-reduce | flops 1408 | bytes 11264
  75.8 1.3 multiply_reduce_fusion.1
  77.1 3.0 divide_convert_fusion
  80.4 33.6 %all-gather.2.cloned.1.call-done = bf16[8,128,1408]{1,0,2:T(8,128)(2,1)} async-done(((bf16[8,128,352]{1,0,2:T(8,128)(2,1)}), bf16[8,128,1408]{1,0,2:T(8,128)(2,1)}) %all-gather.2.cloned.1.call-update) | async-done | bytes 2883600 | tf_op jit(solution)/shard_map/all_gather | solution.py:97
  114.0 4.8 %copy.19 = bf16[8,128,1408]{2,1,0:T(8,128)(2,1)} copy(bf16[8,128,1408]{1,0,2:T(8,128)(2,1)} %all-gather.2.cloned.1.call-done) | data formatting | bytes 5767168
  118.8 175.5 %while.50 = (s32[]{:T(128)}, f32[8,352,128]{2,1,0:T(8,128)S(1)}, s32[8]{0:T(128)S(1)}, s32[8]{0:T(128)S(1)}, s32[8,8,1408]{2,1,0:T(8,128)}, /*index=5*/s32[8,8,5...) while((s32[]{:T(128)}, f32[8,352,128]{2,1,0:T(8,128)S(1)}, ...), condition=%wide.region_5.6_spmd.clone.clone, body=%wide.region_1.5_spmd.sunk.clone.clone.sunk | while | flops 135466512 | bytes 3946544 | solution.py:112
  125.5 15.2 %while.51 = (s32[]{:T(128)}, f32[352,128]{1,0:T(8,128)S(1)}, s32[8,1408]{1,0:T(8,128)S(1)}, s32[]{:T(128)}, bf16[352,1408]{1,0:T(8,128)(2,1)S(1)}, /*index=5*/s3...) while((s32[]{:T(128)}, f32[352,128]{1,0:T(8,128)S(1)}, ...), condition=%wide.region_4.4_spmd.clone.clone, body=%wide.region_2.0_spmd.sunk.clone.clone.sunk | while | flops 131005960 | bytes 1768713 | solution.py:76
  147.4 15.2 %while.51 = (s32[]{:T(128)}, f32[352,128]{1,0:T(8,128)S(1)}, s32[8,1408]{1,0:T(8,128)S(1)}, s32[]{:T(128)}, bf16[352,1408]{1,0:T(8,128)(2,1)S(1)}, /*index=5*/s3...) while((s32[]{:T(128)}, f32[352,128]{1,0:T(8,128)S(1)}, ...), condition=%wide.region_4.4_spmd.clone.clone, body=%wide.region_2.0_spmd.sunk.clone.clone.sunk | while | flops 131005960 | bytes 1768713 | solution.py:76
  169.4 15.2 %while.51 = (s32[]{:T(128)}, f32[352,128]{1,0:T(8,128)S(1)}, s32[8,1408]{1,0:T(8,128)S(1)}, s32[]{:T(128)}, bf16[352,1408]{1,0:T(8,128)(2,1)S(1)}, /*index=5*/s3...) while((s32[]{:T(128)}, f32[352,128]{1,0:T(8,128)S(1)}, ...), condition=%wide.region_4.4_spmd.clone.clone, body=%wide.region_2.0_spmd.sunk.clone.clone.sunk | while | flops 131005960 | bytes 1768713 | solution.py:76
  191.3 15.2 %while.51 = (s32[]{:T(128)}, f32[352,128]{1,0:T(8,128)S(1)}, s32[8,1408]{1,0:T(8,128)S(1)}, s32[]{:T(128)}, bf16[352,1408]{1,0:T(8,128)(2,1)S(1)}, /*index=5*/s3...) while((s32[]{:T(128)}, f32[352,128]{1,0:T(8,128)S(1)}, ...), condition=%wide.region_4.4_spmd.clone.clone, body=%wide.region_2.0_spmd.sunk.clone.clone.sunk | while | flops 131005960 | bytes 1768713 | solution.py:76
  213.2 15.2 %while.51 = (s32[]{:T(128)}, f32[352,128]{1,0:T(8,128)S(1)}, s32[8,1408]{1,0:T(8,128)S(1)}, s32[]{:T(128)}, bf16[352,1408]{1,0:T(8,128)(2,1)S(1)}, /*index=5*/s3...) while((s32[]{:T(128)}, f32[352,128]{1,0:T(8,128)S(1)}, ...), condition=%wide.region_4.4_spmd.clone.clone, body=%wide.region_2.0_spmd.sunk.clone.clone.sunk | while | flops 131005960 | bytes 1768713 | solution.py:76
  235.2 15.2 %while.51 = (s32[]{:T(128)}, f32[352,128]{1,0:T(8,128)S(1)}, s32[8,1408]{1,0:T(8,128)S(1)}, s32[]{:T(128)}, bf16[352,1408]{1,0:T(8,128)(2,1)S(1)}, /*index=5*/s3...) while((s32[]{:T(128)}, f32[352,128]{1,0:T(8,128)S(1)}, ...), condition=%wide.region_4.4_spmd.clone.clone, body=%wide.region_2.0_spmd.sunk.clone.clone.sunk | while | flops 131005960 | bytes 1768713 | solution.py:76
  257.1 15.2 %while.51 = (s32[]{:T(128)}, f32[352,128]{1,0:T(8,128)S(1)}, s32[8,1408]{1,0:T(8,128)S(1)}, s32[]{:T(128)}, bf16[352,1408]{1,0:T(8,128)(2,1)S(1)}, /*index=5*/s3...) while((s32[]{:T(128)}, f32[352,128]{1,0:T(8,128)S(1)}, ...), condition=%wide.region_4.4_spmd.clone.clone, body=%wide.region_2.0_spmd.sunk.clone.clone.sunk | while | flops 131005960 | bytes 1768713 | solution.py:76
  279.0 15.2 %while.51 = (s32[]{:T(128)}, f32[352,128]{1,0:T(8,128)S(1)}, s32[8,1408]{1,0:T(8,128)S(1)}, s32[]{:T(128)}, bf16[352,1408]{1,0:T(8,128)(2,1)S(1)}, /*index=5*/s3...) while((s32[]{:T(128)}, f32[352,128]{1,0:T(8,128)S(1)}, ...), condition=%wide.region_4.4_spmd.clone.clone, body=%wide.region_2.0_spmd.sunk.clone.clone.sunk | while | flops 131005960 | bytes 1768713 | solution.py:76
  295.6 1.1 collective-permute-done
  296.8 1.5 collective-permute-start.1
  298.3 2.1 collective-permute-done.1
  300.4 3.0 collective-permute-start.2
  303.4 2.1 collective-permute-done.2
  305.4 1.5 collective-permute-start.3
  306.9 2.1 collective-permute-done.3
  309.0 3.0 collective-permute-start.4
  312.6 63.4 %psum.7 = f32[]{:T(128)} all-reduce(f32[]{:T(128)} %convert_reduce_fusion), channel_id=1, replica_groups=mesh['board'=32,'hand'=4] {'board'}, use_global_device_ids=true, to_apply=%region_9.10 | all-reduce | flops 1 | bytes 8 | tf_op jit(solution)/shard_map/psum | solution.py:84
  376.0 1.3 add_divide_fusion
  (554 shorter events, 116.3 us)
Async XLA Ops:
  6.5 73.6 %copy-start = (s32[1408]{0:T(1024)S(1)}, s32[1408]{0:T(1024)}, u32[]{:S(2)}) copy-start(s32[1408]{0:T(1024)} %constant.188.clone) | copy-start | bytes 16900
  6.5 73.7 %copy-start.1 = (s32[1408]{0:T(1024)S(1)}, s32[1408]{0:T(1024)}, u32[]{:S(2)}) copy-start(s32[1408]{0:T(1024)} %constant.189.clone) | copy-start | bytes 16900
  6.5 73.8 %copy-start.3 = (s32[8]{0:T(128)S(1)}, s32[8]{0:T(128)}, u32[]{:S(2)}) copy-start(s32[8]{0:T(128)} %param.19) | copy-start | bytes 100
  6.5 73.8 %copy-start.6 = (s32[8]{0:T(128)S(1)}, s32[8]{0:T(128)}, u32[]{:S(2)}) copy-start(s32[8]{0:T(128)} %param.20) | copy-start | bytes 100
  6.5 107.4 %all-gather.2.cloned.1.call-start = ((), (), s32[]{:S(2)}) async-start(), calls=%async_computation | async-start | bytes 3604480 | tf_op jit(solution)/shard_map/all_gather | solution.py:97
  80.3 38.5 %copy-start.2 = (f32[1408]{0:T(1024)S(1)}, f32[1408]{0:T(1024)}, u32[]{:S(2)}) copy-start(f32[1408]{0:T(1024)} %constant.190.clone) | copy-start | bytes 16900
  118.8 175.5 %copy-start.4 = (f32[128]{0:T(128)S(1)}, f32[128]{0:T(128)}, u32[]{:S(2)}) copy-start(f32[128]{0:T(128)} %param.21) | copy-start | bytes 1540
  118.8 175.5 %copy-start.5 = (s32[128]{0:T(128)S(1)}, s32[128]{0:T(128)}, u32[]{:S(2)}) copy-start(s32[128]{0:T(128)} %param.22) | copy-start | bytes 1540
  295.5 1.2 collective-permute-start
  296.8 3.6 collective-permute-start.1
  300.4 5.1 %collective-permute-start.2 = (f32[352]{0:T(512)S(1)}, f32[352]{0:T(512)S(1)}, u32[]{:S(2)}, u32[]{:S(2)}) collective-permute-start(f32[352]{0:T(512)S(1)} %add.111), channel_id=1, source_target_pairs={{0,16},{4,20},{8,24},{12,28},{16,0},{20,4},{24,8},{28,12},{32,48},... | collective-permute-start | bytes 4232 | tf_op jit(solution)/shard_map/ppermute | solution.py:121
  305.4 3.6 collective-permute-start.3
  309.0 67.0 %collective-permute-start.4 = (f32[352]{0:T(512)S(1)}, f32[352]{0:T(512)S(1)}, u32[]{:S(2)}, u32[]{:S(2)}) collective-permute-start(f32[352]{0:T(512)S(1)} %add.113), channel_id=1, source_target_pairs={{0,64},{4,68},{8,72},{12,76},{16,80},{20,84},{24,88},{28,92},{32,9... | collective-permute-start | bytes 4232 | tf_op jit(solution)/shard_map/ppermute | solution.py:121
Sparse Core Ops, SparseCore 0:
  80.3 33.6 all-gather.1
